TPU v7x, 256 devices: a whole 4x4x8 slice. The times are simulated.
256 devices in a mesh: dp: 4 (over y_lo, core), tm: 4 (over x), rows: 16 (over z, y_hi).
Axes of the slice: x: 4, y: 4 (y_hi: 2, y_lo: 2; y = y_hi * 2 + y_lo), z: 8, core: 2. Of those that a mesh axis runs over, the one named last changes fastest.
Arguments:
- latents: bfloat16 [4, 8, 16, 30, 512], P('dp', 'tm', 'rows'), may hold values from -6 to 6
- grad_out: bfloat16 [4, 8, 32, 60, 256], P('dp', 'tm', 'rows'), may hold values from -6 to 6
- kernel: bfloat16 [3, 3, 3, 512, 256], replicated, may hold values from -0.0546875 to 0.0546875
Outputs:
- grad_latents: bfloat16 [4, 8, 16, 30, 512], P('dp', 'tm', 'rows')
- weight_grad: float32 [512, 3, 3, 3, 256], P(('dp', 'tm', 'rows'))
All inputs are finite; a program needn't handle non-finite values.
Results may differ from a plain program's by a relative error of at most 0.001.
Values may be sent and summed in bfloat16 or wider, within the bound.
A program may use at most 128 MiB of HBM per device.

v0:
```python
import jax
import jax.numpy as jnp
from jax import lax
from jax.sharding import PartitionSpec as P


def shift_from(shard, axis, by):
    peers = lax.axis_size(axis)
    pairs = [(i, i + by) for i in range(peers) if 0 <= i + by < peers]
    return lax.ppermute(shard, axis, pairs)


def pool_pairs(values, dim):
    n = values.shape[dim] // 2
    pad = [(0, 0)] * values.ndim
    pad[dim] = (1, 1)
    ext = jnp.pad(values, pad)
    shape = values.shape
    shifted = ext.reshape(shape[:dim] + (n + 1, 2) + shape[dim + 1 :]).sum(axis=dim + 1)
    aligned = values.reshape(shape[:dim] + (n, 2) + shape[dim + 1 :]).sum(axis=dim + 1)
    out = [
        lax.slice_in_dim(shifted, 1, n + 1, axis=dim),
        aligned,
        lax.slice_in_dim(shifted, 0, n, axis=dim),
    ]
    return jnp.stack(out, axis=dim + 1)


def with_halo(block, axis, dim, width):
    count = lax.axis_size(axis)
    forward = [(i, i + 1) for i in range(count - 1)]
    backward = [(target, source) for source, target in forward]
    low = lax.ppermute(
        lax.slice_in_dim(block, block.shape[dim] - width, None, axis=dim), axis, forward
    )
    high = lax.ppermute(lax.slice_in_dim(block, 0, width, axis=dim), axis, backward)
    return jnp.concatenate([low, block, high], axis=dim)


def body(latents, grad_out, kernel):
    frames = grad_out.shape[1]
    height = grad_out.shape[2]
    width = grad_out.shape[3]
    channels = latents.shape[4]
    outputs = grad_out.shape[4]
    devices = lax.axis_size("dp") * lax.axis_size("tm") * lax.axis_size("rows")
    factor = float(devices * frames * height * width) ** (-0.5)
    slab_count = lax.axis_size("rows")
    grad_whole = lax.all_gather(grad_out[0], "rows", axis=1, tiled=True)
    whole_height = grad_whole.shape[1]
    near = with_halo(grad_out[0], "rows", 1, 1)
    later = shift_from(near, "tm", -1)
    grad_all = jnp.concatenate([near, later], axis=0)
    grad_all = jnp.pad(grad_all, ((0, 0), (0, 0), (1, 1), (0, 0)))
    patches = []
    for a in range(3):
        for i in range(3):
            for j in range(3):
                patches.append(
                    grad_all[2 - a : 2 - a + frames, 2 - i : 2 - i + height, 2 - j : 2 - j + width]
                )
    patches = jnp.stack(patches, axis=3).reshape(frames * height * width, 27, outputs)
    grad_up = lax.dot_general(
        patches,
        kernel.reshape(27, channels, outputs),
        (((1, 2), (0, 2)), ((), ())),
        preferred_element_type=jnp.float32,
    )
    pooled = grad_up.reshape(frames, height // 2, 2, width // 2, 2, channels).sum(axis=(2, 4))
    grad_latents = pooled.astype(jnp.bfloat16)[None]
    groups = lax.axis_size("dp") * lax.axis_size("tm")
    share = channels // devices
    earlier = shift_from(latents, "tm", 1)
    with_earlier = jnp.concatenate([earlier, latents], axis=1)
    lead = with_earlier.shape[:4]
    regrouped = with_earlier.reshape(lead + (groups, slab_count, share))
    regrouped = jnp.swapaxes(regrouped, 4, 5).reshape(lead + (channels,))
    owned = lax.all_to_all(regrouped, "rows", split_axis=4, concat_axis=2, tiled=True)[0]
    group_channels = owned.shape[3]
    taps_a = jnp.stack([owned[a : a + frames] for a in range(3)], axis=0)
    pooled_grad = pool_pairs(pool_pairs(grad_whole.astype(jnp.float32), 1), 3)
    scaled = pooled_grad * 65537.0
    top = scaled - (scaled - pooled_grad)
    both = jnp.stack([top, pooled_grad - top], axis=0).astype(jnp.bfloat16)
    term = jnp.einsum("afrsc,xfrisjo->caijxo", taps_a, both, preferred_element_type=jnp.float32)
    term = (term[..., 0, :] + term[..., 1, :]) * factor
    term = term.reshape(group_channels, 3, 3, 3, outputs)
    term = lax.psum_scatter(term, "dp", scatter_dimension=0, tiled=True)
    weight_grad = lax.psum_scatter(term, "tm", scatter_dimension=0, tiled=True)
    return (grad_latents, weight_grad)


def solution(mesh):
    in_specs = (P("dp", "tm", "rows", None, None), P("dp", "tm", "rows", None, None), P())
    out_specs = (P("dp", "tm", "rows", None, None), P(("dp", "tm", "rows"), None, None, None, None))
    return jax.shard_map(body, mesh=mesh, in_specs=in_specs, out_specs=out_specs, check_vma=False)
```

profile of v0, /device:TPU:8, one launch (start us, length us, event | category | flops | bytes accessed | tf_op | source)
XLA Modules:
  0.0 247.5 jit_solution(9366353959574920145)
XLA Ops:
  7.2 3.4 %collective-permute-start.3 = (bf16[1,2,1,30,512]{4,1,3,2,0:T(2,128)(2,1)}, bf16[1,2,1,30,512]{4,1,3,2,0:T(2,128)(2,1)S(1)}, u32[]{:S(2)}, u32[]{:S(2)}) collective-permute-start(bf16[1,2,1,30,512]{4,1,3,2,0:T(2,128)(2,1)} %param.3), channel_id=1, source_target_pairs={{0,16},{16,32},{32,48},{1,17},{17,33},{33,49},{2,18},{18,34},{34,5... | collective-permute-start | bytes 184328 | tf_op jit(solution)/shard_map/ppermute | solution.py:10
  10.6 1.2 fusion.25
  11.8 4.2 %collective-permute-start = (bf16[2,1,60,256]{3,1,2,0:T(2,128)(2,1)S(1)}, bf16[2,1,60,256]{3,1,2,0:T(2,128)(2,1)S(1)}, u32[]{:S(2)}, u32[]{:S(2)}) collective-permute-start(bf16[2,1,60,256]{3,1,2,0:T(2,128)(2,1)S(1)} %get-tuple-element.46), channel_id=1, source_target_pairs={{0,1},{1,2},{2,3},{3,4},{4,5},{5,6},{6,7},{7,8},{8,9},{9,10},{10,1... | collective-permute-start | bytes 184328 | tf_op jit(solution)/shard_map/ppermute | solution.py:33
  16.0 1.3 collective-permute-start.1
  17.3 1.6 copy.102
  19.0 1.3 dynamic-slice
  20.9 1.0 pad_maximum_fusion.5
  23.0 1.6 reshape.353
  24.7 12.5 %all-to-all-start = ((bf16[16,2,1920]{2,1,0:T(2,128)(2,1)}), bf16[16,2,1920]{2,1,0:T(2,128)(2,1)S(1)}, u32[]{:S(2)}, u32[]{:S(2)}) async-start(bf16[16,2,1920]{2,1,0:T(2,128)(2,1)} %reshape.353), calls=%async_computation | async-start | bytes 245760 | tf_op jit(solution)/shard_map/all_to_all | solution.py:78
  37.7 1.7 collective-permute-start.2
  39.9 8.4 %all-to-all-done = bf16[16,2,1920]{2,1,0:T(2,128)(2,1)S(1)} async-done(((bf16[16,2,1920]{2,1,0:T(2,128)(2,1)}), bf16[16,2,1920]{2,1,0:T(2,128)(2,1)S(1)}, u32[]{:S(2)}, u32[]{:S(2)}) %all-to-all-start) | async-done | bytes 122912 | tf_op jit(solution)/shard_map/all_to_all | solution.py:78
  48.4 1.4 reshape.354
  49.8 0.9 slice_bitcast_fusion.2
  51.4 0.7 pad_slice_fusion
  52.1 0.7 copy_dynamic-update-slice_fusion.26
  54.4 0.7 copy_dynamic-update-slice_fusion.23
  55.8 0.7 copy_dynamic-update-slice_fusion.21
  59.2 1.6 pad_slice_fusion.1
  61.5 0.7 copy_dynamic-update-slice_fusion.15
  62.8 0.7 copy_dynamic-update-slice_fusion.13
  64.2 0.7 copy_dynamic-update-slice_fusion.11
  64.9 0.7 copy_dynamic-update-slice_fusion.10
  66.3 0.7 copy_dynamic-update-slice_fusion.8
  66.9 41.3 %all-gather.3.cloned.1.call-done = bf16[1,2,32,60,256]{4,1,3,0,2:T(2,128)(2,1)} async-done(((bf16[1,2,2,60,256]{4,1,3,0,2:T(2,128)(2,1)}), bf16[1,2,32,60,256]{4,1,3,0,2:T(2,128)(2,1)}) %all-gather.3.cloned.1.call-update) | async-done | bytes 1966096 | tf_op jit(solution)/shard_map/all_gather | solution.py:49
  108.2 2.9 %convert_bitcast_fusion = f32[2,32,60,256]{3,0,2,1:T(2,128)S(1)} fusion(bf16[1,2,32,60,256]{4,1,3,0,2:T(2,128)(2,1)} %all-gather.3.cloned.1.call-done), kind=kLoop, calls=%fused_computation.21 | loop fusion | flops 983040 | bytes 5898240 | tf_op jit(solution)/shard_map/convert_element_type | solution.py:81
  111.1 3.4 %pad.13 = f32[2,34,60,256]{3,0,2,1:T(2,128)} pad(f32[2,32,60,256]{3,0,2,1:T(2,128)S(1)} %convert_bitcast_fusion, f32[]{:T(128)} %constant.3.clone.1), padding=0_0x1_1x0_0x0_0 | pad | bytes 8110084 | tf_op jit(solution)/shard_map/jit(_pad)/pad | solution.py:17
  114.5 5.3 %reduce_sum.46 = f32[2,17,60,256]{3,0,2,1:T(2,128)S(1)} reduce(f32[2,17,2,60,256]{4,0,3,2,1:T(2,128)} %bitcast.115, f32[]{:T(128)} %constant.3.clone.1), dimensions={2}, to_apply=%region_1.2 | reduce | flops 522240 | bytes 6266884 | tf_op jit(solution)/shard_map/reduce_sum | solution.py:19
  119.8 16.3 %fusion.23 = (f32[2,16,60,256]{3,0,2,1:T(2,128)}, f32[2,16,1,60,256]{4,0,3,1,2:T(2,128)}, f32[2,16,1,60,256]{4,0,3,1,2:T(2,128)}, f32[2,16,60,256]{3,0,2,1:T(2,128)}) fusion(f32[2,17,60,256]{3,0,2,1:T(2,128)S(1)} %reduce_sum.46), kind=kLoop, calls=%fused_computation.89 | loop fusion | bytes 11796480 | tf_op jit(solution)/shard_map/slice | solution.py:22
  136.1 4.7 %reduce_sum.47 = f32[2,16,60,256]{3,0,2,1:T(2,128)S(1)} reduce(bf16[2,16,2,60,256]{4,0,3,2,1:T(2,128)(2,1)} %bitcast.117, f32[]{:T(128)} %constant.3.clone.1), dimensions={2}, to_apply=%region_2.3 | reduce | flops 491520 | bytes 3932164 | tf_op jit(solution)/shard_map/reduce_sum | solution.py:20
  140.9 1.9 copy.106
  142.7 1.0 copy-done.4
  143.7 5.5 %select_maximum_fusion = f32[2,16,3,62,256]{4,0,3,1,2:T(2,128)} fusion(f32[2,16,1,60,256]{4,0,3,1,2:T(2,128)S(1)} %copy-done.4, f32[2,16,1,60,256]{4,0,3,1,2:T(2,128)S(1)} %bitcast.114, f32[2,16,1,60,256]{4,0,3,1,2:T(2,128)S(1)} %copy-done.3), kind=kLoop, calls=%fused_computation.10 | loop fusion | flops 12189696 | bytes 11993088 | tf_op jit(solution)/shard_map/stack | solution.py:26
  149.2 7.7 %reduce.2 = f32[2,16,3,31,256]{4,0,3,1,2:T(2,128)S(1)} reduce(f32[2,16,3,31,2,256]{5,0,4,3,1,2:T(2,128)} %bitcast.113, f32[]{:T(128)} %constant.3.clone.1), dimensions={4}, to_apply=%region_3.4 | reduce | flops 761856 | bytes 9142276
  156.9 1.5 fusion.22
  159.1 0.9 copy-done
  160.7 0.9 maximum_reduce_fusion
  161.5 1.7 copy.159
  163.2 1.0 copy_bitcast_fusion
  164.2 2.2 fusion.1
  166.5 1.7 fusion.8
  168.3 1.1 fusion.16
  171.5 0.7 copy_dynamic-update-slice_fusion.4
  172.2 0.7 copy_dynamic-update-slice_fusion.3
  174.9 12.6 %reduce-scatter.3.cloned.1.call-done = f32[8,3,3,3,256]{4,0,1,3,2:T(8,128)} async-done(((f32[32,3,3,3,256]{4,0,1,3,2:T(8,128)}), f32[8,3,3,3,256]{4,0,1,3,2:T(8,128)}) %reduce-scatter.3.cloned.1.call-update) | async-done | bytes 221200 | tf_op jit(solution)/shard_map/reduce_scatter | solution.py:88
  187.6 6.1 %fusion.12 = bf16[2,30,512]{2,1,0:T(8,128)(2,1)S(1)} fusion(bf16[27,512,256,1,1,1]{2,1,0,5,4,3:T(8,128)(2,1)} %bitcast.158, bf16[2,1,2,30,2,27,256]{6,3,5,4,2,0,1:T(8,128)(2,1)} %copy_dynamic-update-slice_fusion), kind=kOutput, calls=%fused_computation.20 | convolution fusion | flops 1698785280 | bytes 10457088 | tf_op jit(solution)/shard_map/dot_general | solution.py:63
  193.7 0.7 copy.114
  194.4 44.7 %all-reduce.6.cloned.1.call-done = f32[8,3,3,3,256]{4,0,1,3,2:T(8,128)} async-done(((f32[8,3,3,3,256]{4,0,1,3,2:T(8,128)}), f32[8,3,3,3,256]{4,0,1,3,2:T(8,128)}) %all-reduce.6.cloned.1.call-update) | async-done | bytes 221200
  239.1 1.0 constant_dynamic-slice_fusion
  (63 shorter events, 16.6 us)
Async XLA Ops:
  7.2 30.1 %copy-start.5 = (bf16[1,2,2,60,256]{4,2,3,1,0:T(2,128)(2,1)S(1)}, bf16[1,2,2,60,256]{4,2,3,1,0:T(2,128)(2,1)}, u32[]{:S(2)}) copy-start(bf16[1,2,2,60,256]{4,2,3,1,0:T(2,128)(2,1)} %param.4) | copy-start | bytes 368644
  7.2 101.0 %all-gather.3.cloned.1.call-start = ((), (), s32[]{:S(2)}) async-start(), calls=%async_computation.3 | async-start | bytes 2088960 | tf_op jit(solution)/shard_map/all_gather | solution.py:49
  7.2 13.7 %collective-permute-start.3 = (bf16[1,2,1,30,512]{4,1,3,2,0:T(2,128)(2,1)}, bf16[1,2,1,30,512]{4,1,3,2,0:T(2,128)(2,1)S(1)}, u32[]{:S(2)}, u32[]{:S(2)}) collective-permute-start(bf16[1,2,1,30,512]{4,1,3,2,0:T(2,128)(2,1)} %param.3), channel_id=1, source_target_pairs={{0,16},{16,32},{32,48},{1,17},{17,33},{33,49},{2,18},{18,34},{34,5... | collective-permute-start | bytes 184328 | tf_op jit(solution)/shard_map/ppermute | solution.py:10
  11.8 25.4 %collective-permute-start = (bf16[2,1,60,256]{3,1,2,0:T(2,128)(2,1)S(1)}, bf16[2,1,60,256]{3,1,2,0:T(2,128)(2,1)S(1)}, u32[]{:S(2)}, u32[]{:S(2)}) collective-permute-start(bf16[2,1,60,256]{3,1,2,0:T(2,128)(2,1)S(1)} %get-tuple-element.46), channel_id=1, source_target_pairs={{0,1},{1,2},{2,3},{3,4},{4,5},{5,6},{6,7},{7,8},{8,9},{9,10},{10,1... | collective-permute-start | bytes 184328 | tf_op jit(solution)/shard_map/ppermute | solution.py:33
  16.0 21.2 %collective-permute-start.1 = (bf16[2,1,60,256]{3,1,2,0:T(2,128)(2,1)S(1)}, bf16[2,1,60,256]{3,1,2,0:T(2,128)(2,1)S(1)}, u32[]{:S(2)}, u32[]{:S(2)}) collective-permute-start(bf16[2,1,60,256]{3,1,2,0:T(2,128)(2,1)S(1)} %get-tuple-element.47), channel_id=1, source_target_pairs={{1,0},{2,1},{3,2},{4,3},{5,4},{6,5},{7,6},{8,7},{9,8},{10,9},{11,1... | collective-permute-start | bytes 184328 | tf_op jit(solution)/shard_map/ppermute | solution.py:36
  24.7 23.7 %all-to-all-start = ((bf16[16,2,1920]{2,1,0:T(2,128)(2,1)}), bf16[16,2,1920]{2,1,0:T(2,128)(2,1)S(1)}, u32[]{:S(2)}, u32[]{:S(2)}) async-start(bf16[16,2,1920]{2,1,0:T(2,128)(2,1)} %reshape.353), calls=%async_computation | async-start | bytes 245760 | tf_op jit(solution)/shard_map/all_to_all | solution.py:78
  37.2 150.3 %reduce-scatter.3.cloned.1.call-start = ((), (), s32[]{:S(2)}) async-start(), calls=%async_computation.2 | async-start | bytes 1105920 | tf_op jit(solution)/shard_map/reduce_scatter | solution.py:88
  37.7 13.0 %collective-permute-start.2 = (bf16[2,4,60,256]{3,1,2,0:T(4,128)(2,1)S(1)}, bf16[2,4,60,256]{3,1,2,0:T(4,128)(2,1)S(1)}, u32[]{:S(2)}, u32[]{:S(2)}) collective-permute-start(bf16[2,4,60,256]{3,1,2,0:T(4,128)(2,1)S(1)} %pad_maximum_fusion.2), channel_id=1, source_target_pairs={{16,0},{32,16},{48,32},{17,1},{33,17},{49,33},{18,2},{34,18},{50,3... | collective-permute-start | bytes 737288 | tf_op jit(solution)/shard_map/ppermute | solution.py:10
  140.8 1.9 copy-start.3
  140.8 2.8 %copy-start.4 = (f32[2,16,1,60,256]{4,0,3,1,2:T(2,128)S(1)}, f32[2,16,1,60,256]{4,0,3,1,2:T(2,128)}, u32[]{:S(2)}) copy-start(f32[2,16,1,60,256]{4,0,3,1,2:T(2,128)} %get-tuple-element.16) | copy-start | bytes 5898244
  156.9 1.6 copy-start.1
  158.5 1.5 copy-start
  158.5 2.2 copy-start.2
  164.2 2.3 copy-start.10
  164.2 2.3 copy-start.11
  164.2 2.3 copy-start.12
  168.2 1.9 copy-start.9
  168.2 2.5 %copy-start.8 = (bf16[2,2,60,256]{3,1,2,0:T(2,128)(2,1)S(1)}, bf16[2,2,60,256]{3,1,2,0:T(2,128)(2,1)}, u32[]{:S(2)}) copy-start(bf16[2,2,60,256]{3,1,2,0:T(2,128)(2,1)} %get-tuple-element.37) | copy-start | bytes 368644
  168.2 3.9 %copy-start.7 = (bf16[2,2,60,256]{3,1,2,0:T(2,128)(2,1)S(1)}, bf16[2,2,60,256]{3,1,2,0:T(2,128)(2,1)}, u32[]{:S(2)}) copy-start(bf16[2,2,60,256]{3,1,2,0:T(2,128)(2,1)} %get-tuple-element.38) | copy-start | bytes 368644
  168.3 4.6 %copy-start.6 = (bf16[2,2,60,256]{3,1,2,0:T(2,128)(2,1)S(1)}, bf16[2,2,60,256]{3,1,2,0:T(2,128)(2,1)}, u32[]{:S(2)}) copy-start(bf16[2,2,60,256]{3,1,2,0:T(2,128)(2,1)} %get-tuple-element.31) | copy-start | bytes 368644
  169.4 69.7 %all-reduce.6.cloned.1.call-start = ((), (), s32[]{:S(2)}) async-start(), calls=%async_computation.4 | async-start | bytes 442368
Sparse Core Ops, SparseCore 0:
  19.1 89.0 all-gather.2
  169.5 17.9 reduce-scatter.2
  189.9 49.1 all-reduce.5
where the time goes:
time: 251 us; the launch traced here: 247 us
  waiting for transfers between devices  107 us (43%)
  local copies, waits for them, and re-layouts  61.5 us (25%)
  other arithmetic  32.8 us (13%)
  starting transfers between devices  23.2 us (9%)
  between operations  15 us (6%)
  matrix products  7.87 us (3%)
    unnamed x4, waiting for transfers between devices  44.8 us
    all_gather x1, waiting for transfers between devices, body(): grad_whole = lax.all_gather(grad_out[0], 'rows', axis=1, tiled=True)  41.3 us
    unnamed x59, local copies, waits for them, and re-layouts  27.8 us
    slice x3, local copies, waits for them, and re-layouts, pool_pairs(): lax.slice_in_dim(shifted, 1, n + 1, axis=dim)  18.5 us
    reduce_scatter x1, waiting for transfers between devices, body(): term = lax.psum_scatter(term, 'dp', scatter_dimension=0, tiled=True)  12.6 us
    all_to_all x1, starting transfers between devices, body(): lax.all_to_all(regrouped, 'rows', split_axis=4, concat_axis=2, tiled=True)  12.5 us
    all_to_all x1, waiting for transfers between devices, body(): lax.all_to_all(regrouped, 'rows', split_axis=4, concat_axis=2, tiled=True)  8.43 us
    unnamed x1, other arithmetic  7.74 us
  transfers between devices with their start and end apart: 8, of which 4 were waited for; matrix products, arithmetic and copies ran while one was open for 16% of the time, Pallas kernels for 0%

commit v1 on v0

--- a/solution.py
+++ b/solution.py
@@ -2,6 +2,19 @@
 import jax.numpy as jnp
 from jax import lax
 from jax.sharding import PartitionSpec as P
+
+
+def scan_links(vector, mesh_name):
+    long_array = jnp.concatenate(
+        jax.lax.all_to_all(
+            jnp.stack(jnp.split(vector, jax.lax.axis_size(mesh_name), axis=4), axis=0),
+            mesh_name,
+            0,
+            0,
+        ),
+        axis=2,
+    )
+    return long_array
 
 
 def shift_from(shard, axis, by):
@@ -75,7 +88,7 @@
     lead = with_earlier.shape[:4]
     regrouped = with_earlier.reshape(lead + (groups, slab_count, share))
     regrouped = jnp.swapaxes(regrouped, 4, 5).reshape(lead + (channels,))
-    owned = lax.all_to_all(regrouped, "rows", split_axis=4, concat_axis=2, tiled=True)[0]
+    owned = scan_links(regrouped, "rows")[0]
     group_channels = owned.shape[3]
     taps_a = jnp.stack([owned[a : a + frames] for a in range(3)], axis=0)
     pooled_grad = pool_pairs(pool_pairs(grad_whole.astype(jnp.float32), 1), 3)

time: 251 us -> 236 us (0.940); the launches traced: 247 us -> 236 us
  local copies, waits for them, and re-layouts: 61.5 us -> 48.7 us
    slice x3, local copies, waits for them, and re-layouts: 18.5 us -> 6.54 us  [pool_pairs(): lax.slice_in_dim(shifted, 1, n + 1, axis=dim)]
    unnamed x59 -> x74, local copies, waits for them, and re-layouts: 27.8 us -> 26.3 us
where the time goes in v1:
time: 236 us
  waiting for transfers between devices  108 us (46%)
  local copies, waits for them, and re-layouts  48.7 us (21%)
  other arithmetic  32.8 us (14%)
  starting transfers between devices  23.5 us (10%)
  between operations  14.8 us (6%)
  matrix products  7.87 us (3%)
    unnamed x4, waiting for transfers between devices  44.8 us
    all_gather x1, waiting for transfers between devices, body(): grad_whole = lax.all_gather(grad_out[0], 'rows', axis=1, tiled=True)  41.9 us
    unnamed x74, local copies, waits for them, and re-layouts  26.3 us
    reduce_scatter x1, waiting for transfers between devices, body(): term = lax.psum_scatter(term, 'dp', scatter_dimension=0, tiled=True)  12.7 us
    all_to_all x1, starting transfers between devices, scan_links(): jax.lax.all_to_all(jnp.stack(jnp.split(vector, jax.lax.axis_size(mesh_nam...  11.2 us
    all_to_all x1, waiting for transfers between devices, scan_links(): jax.lax.all_to_all(jnp.stack(jnp.split(vector, jax.lax.axis_size(mesh_nam...  8.63 us
    unnamed x1, other arithmetic  7.74 us
    slice x3, local copies, waits for them, and re-layouts, pool_pairs(): lax.slice_in_dim(shifted, 1, n + 1, axis=dim)  6.54 us
  transfers between devices with their start and end apart: 8, of which 4 were waited for; matrix products, arithmetic and copies ran while one was open for 16% of the time, Pallas kernels for 0%

profile of v1, /device:TPU:8, one launch (start us, length us, event | category | flops | bytes accessed | tf_op | source)
XLA Modules:
  0.0 235.7 jit_solution(4671794044894006566)
XLA Ops:
  7.2 3.4 %collective-permute-start.3 = (bf16[1,2,1,30,512]{4,1,3,2,0:T(2,128)(2,1)}, bf16[1,2,1,30,512]{4,1,3,2,0:T(2,128)(2,1)S(1)}, u32[]{:S(2)}, u32[]{:S(2)}) collective-permute-start(bf16[1,2,1,30,512]{4,1,3,2,0:T(2,128)(2,1)} %param.3), channel_id=1, source_target_pairs={{0,16},{16,32},{32,48},{1,17},{17,33},{33,49},{2,18},{18,34},{34,5... | collective-permute-start | bytes 184328 | tf_op jit(solution)/shard_map/ppermute | solution.py:23
  10.6 1.2 fusion.25
  11.8 1.3 collective-permute-start.1
  13.1 6.1 %collective-permute-start = (bf16[2,1,60,256]{3,1,2,0:T(2,128)(2,1)S(1)}, bf16[2,1,60,256]{3,1,2,0:T(2,128)(2,1)S(1)}, u32[]{:S(2)}, u32[]{:S(2)}) collective-permute-start(bf16[2,1,60,256]{3,1,2,0:T(2,128)(2,1)S(1)} %get-tuple-element.46), channel_id=1, source_target_pairs={{0,1},{1,2},{2,3},{3,4},{4,5},{5,6},{6,7},{7,8},{8,9},{9,10},{10,1... | collective-permute-start | bytes 184328 | tf_op jit(solution)/shard_map/ppermute | solution.py:46
  19.2 1.6 copy.138
  20.9 1.3 dynamic-slice
  22.8 1.0 pad_maximum_fusion.5
  25.2 1.2 reshape.356
  26.4 11.2 %all-to-all-start = ((bf16[16,2,1920]{2,1,0:T(2,128)(2,1)}), bf16[16,2,1920]{2,1,0:T(2,128)(2,1)S(1)}, u32[]{:S(2)}, u32[]{:S(2)}) async-start(bf16[16,2,1920]{2,1,0:T(2,128)(2,1)} %reshape.356), calls=%async_computation | async-start | bytes 245760 | tf_op jit(solution)/shard_map/all_to_all | solution.py:9
  38.1 1.5 collective-permute-start.2
  40.1 8.6 %all-to-all-done = bf16[16,2,1920]{2,1,0:T(2,128)(2,1)S(1)} async-done(((bf16[16,2,1920]{2,1,0:T(2,128)(2,1)}), bf16[16,2,1920]{2,1,0:T(2,128)(2,1)S(1)}, u32[]{:S(2)}, u32[]{:S(2)}) %all-to-all-start) | async-done | bytes 122912 | tf_op jit(solution)/shard_map/all_to_all | solution.py:9
  49.5 0.9 slice_bitcast_fusion.2
  51.2 0.7 pad_slice_fusion
  51.9 0.7 copy_dynamic-update-slice_fusion.26
  54.2 0.7 copy_dynamic-update-slice_fusion.23
  55.5 0.7 copy_dynamic-update-slice_fusion.21
  58.9 1.6 pad_slice_fusion.1
  60.5 0.7 copy_dynamic-update-slice_fusion.16
  61.2 0.7 copy_dynamic-update-slice_fusion.15
  62.6 0.7 copy_dynamic-update-slice_fusion.13
  63.9 0.7 copy_dynamic-update-slice_fusion.11
  64.6 0.7 copy_dynamic-update-slice_fusion.10
  66.0 0.7 copy_dynamic-update-slice_fusion.8
  66.7 41.9 %all-gather.3.cloned.1.call-done = bf16[1,2,32,60,256]{4,1,3,0,2:T(2,128)(2,1)} async-done(((bf16[1,2,2,60,256]{4,1,3,0,2:T(2,128)(2,1)}), bf16[1,2,32,60,256]{4,1,3,0,2:T(2,128)(2,1)}) %all-gather.3.cloned.1.call-update) | async-done | bytes 1966096 | tf_op jit(solution)/shard_map/all_gather | solution.py:62
  108.6 2.9 %convert_bitcast_fusion = f32[2,32,60,256]{3,0,2,1:T(2,128)S(1)} fusion(bf16[1,2,32,60,256]{4,1,3,0,2:T(2,128)(2,1)} %all-gather.3.cloned.1.call-done), kind=kLoop, calls=%fused_computation.21 | loop fusion | flops 983040 | bytes 5898240 | tf_op jit(solution)/shard_map/convert_element_type | solution.py:94
  111.5 3.4 %pad.13 = f32[2,34,60,256]{3,0,2,1:T(2,128)} pad(f32[2,32,60,256]{3,0,2,1:T(2,128)S(1)} %convert_bitcast_fusion, f32[]{:T(128)} %constant.3.clone.1), padding=0_0x1_1x0_0x0_0 | pad | bytes 8110084 | tf_op jit(solution)/shard_map/jit(_pad)/pad | solution.py:30
  114.8 5.3 %reduce_sum.46 = f32[2,17,60,256]{3,0,2,1:T(2,128)S(1)} reduce(f32[2,17,2,60,256]{4,0,3,2,1:T(2,128)} %bitcast.175, f32[]{:T(128)} %constant.3.clone.1), dimensions={2}, to_apply=%region_1.2 | reduce | flops 522240 | bytes 6266884 | tf_op jit(solution)/shard_map/reduce_sum | solution.py:32
  120.2 4.4 %fusion.23 = (f32[2,16,60,256]{3,0,2,1:T(2,128)}, f32[2,16,1,60,256]{4,0,3,1,2:T(2,128)}, f32[2,16,1,60,256]{4,0,3,1,2:T(2,128)}, f32[2,16,60,256]{3,0,2,1:T(2,128)}) fusion(f32[2,17,60,256]{3,0,2,1:T(2,128)S(1)} %reduce_sum.46), kind=kLoop, calls=%fused_computation.121 | loop fusion | bytes 11796480 | tf_op jit(solution)/shard_map/slice | solution.py:35
  124.5 4.7 %reduce_sum.47 = f32[2,16,60,256]{3,0,2,1:T(2,128)S(1)} reduce(bf16[2,16,2,60,256]{4,0,3,2,1:T(2,128)(2,1)} %bitcast.177, f32[]{:T(128)} %constant.3.clone.1), dimensions={2}, to_apply=%region_2.3 | reduce | flops 491520 | bytes 3932164 | tf_op jit(solution)/shard_map/reduce_sum | solution.py:33
  129.3 1.9 copy.142
  131.2 1.0 copy-done.4
  132.1 5.5 %select_maximum_fusion = f32[2,16,3,62,256]{4,0,3,1,2:T(2,128)} fusion(f32[2,16,1,60,256]{4,0,3,1,2:T(2,128)S(1)} %copy-done.4, f32[2,16,1,60,256]{4,0,3,1,2:T(2,128)S(1)} %bitcast.174, f32[2,16,1,60,256]{4,0,3,1,2:T(2,128)S(1)} %copy-done.3), kind=kLoop, calls=%fused_computation.10 | loop fusion | flops 12189696 | bytes 11993088 | tf_op jit(solution)/shard_map/stack | solution.py:39
  137.6 7.7 %reduce.2 = f32[2,16,3,31,256]{4,0,3,1,2:T(2,128)S(1)} reduce(f32[2,16,3,31,2,256]{5,0,4,3,1,2:T(2,128)} %bitcast.173, f32[]{:T(128)} %constant.3.clone.1), dimensions={4}, to_apply=%region_3.4 | reduce | flops 761856 | bytes 9142276
  145.3 1.5 fusion.22
  147.6 0.9 copy-done
  149.1 0.9 maximum_reduce_fusion
  150.0 1.7 copy.194
  151.7 1.0 copy_bitcast_fusion
  152.6 2.3 fusion.1
  155.0 1.8 fusion.8
  156.8 1.1 fusion.16
  160.0 0.7 copy_dynamic-update-slice_fusion.4
  160.7 0.7 copy_dynamic-update-slice_fusion.3
  163.4 12.7 %reduce-scatter.3.cloned.1.call-done = f32[8,3,3,3,256]{4,0,1,3,2:T(8,128)} async-done(((f32[32,3,3,3,256]{4,0,1,3,2:T(8,128)}), f32[8,3,3,3,256]{4,0,1,3,2:T(8,128)}) %reduce-scatter.3.cloned.1.call-update) | async-done | bytes 221200 | tf_op jit(solution)/shard_map/reduce_scatter | solution.py:101
  176.1 6.1 %fusion.12 = bf16[2,30,512]{2,1,0:T(8,128)(2,1)S(1)} fusion(bf16[27,512,256,1,1,1]{2,1,0,5,4,3:T(8,128)(2,1)} %bitcast.233, bf16[2,1,2,30,2,27,256]{6,3,5,4,2,0,1:T(8,128)(2,1)} %copy_dynamic-update-slice_fusion), kind=kOutput, calls=%fused_computation.20 | convolution fusion | flops 1698785280 | bytes 10457088 | tf_op jit(solution)/shard_map/dot_general | solution.py:76
  182.2 0.7 copy.150
  182.9 44.7 %all-reduce.6.cloned.1.call-done = f32[8,3,3,3,256]{4,0,1,3,2:T(8,128)} async-done(((f32[8,3,3,3,256]{4,0,1,3,2:T(8,128)}), f32[8,3,3,3,256]{4,0,1,3,2:T(8,128)}) %all-reduce.6.cloned.1.call-update) | async-done | bytes 221200
  227.6 1.0 constant_dynamic-slice_fusion
  (79 shorter events, 16.9 us)
Async XLA Ops:
  7.2 30.5 %copy-start.5 = (bf16[1,2,2,60,256]{4,2,3,1,0:T(2,128)(2,1)S(1)}, bf16[1,2,2,60,256]{4,2,3,1,0:T(2,128)(2,1)}, u32[]{:S(2)}) copy-start(bf16[1,2,2,60,256]{4,2,3,1,0:T(2,128)(2,1)} %param.4) | copy-start | bytes 368644
  7.2 101.4 %all-gather.3.cloned.1.call-start = ((), (), s32[]{:S(2)}) async-start(), calls=%async_computation.3 | async-start | bytes 2088960 | tf_op jit(solution)/shard_map/all_gather | solution.py:62
  7.2 15.6 %collective-permute-start.3 = (bf16[1,2,1,30,512]{4,1,3,2,0:T(2,128)(2,1)}, bf16[1,2,1,30,512]{4,1,3,2,0:T(2,128)(2,1)S(1)}, u32[]{:S(2)}, u32[]{:S(2)}) collective-permute-start(bf16[1,2,1,30,512]{4,1,3,2,0:T(2,128)(2,1)} %param.3), channel_id=1, source_target_pairs={{0,16},{16,32},{32,48},{1,17},{17,33},{33,49},{2,18},{18,34},{34,5... | collective-permute-start | bytes 184328 | tf_op jit(solution)/shard_map/ppermute | solution.py:23
  11.8 25.8 %collective-permute-start.1 = (bf16[2,1,60,256]{3,1,2,0:T(2,128)(2,1)S(1)}, bf16[2,1,60,256]{3,1,2,0:T(2,128)(2,1)S(1)}, u32[]{:S(2)}, u32[]{:S(2)}) collective-permute-start(bf16[2,1,60,256]{3,1,2,0:T(2,128)(2,1)S(1)} %get-tuple-element.47), channel_id=1, source_target_pairs={{1,0},{2,1},{3,2},{4,3},{5,4},{6,5},{7,6},{8,7},{9,8},{10,9},{11,1... | collective-permute-start | bytes 184328 | tf_op jit(solution)/shard_map/ppermute | solution.py:49
  13.1 24.5 %collective-permute-start = (bf16[2,1,60,256]{3,1,2,0:T(2,128)(2,1)S(1)}, bf16[2,1,60,256]{3,1,2,0:T(2,128)(2,1)S(1)}, u32[]{:S(2)}, u32[]{:S(2)}) collective-permute-start(bf16[2,1,60,256]{3,1,2,0:T(2,128)(2,1)S(1)} %get-tuple-element.46), channel_id=1, source_target_pairs={{0,1},{1,2},{2,3},{3,4},{4,5},{5,6},{6,7},{7,8},{8,9},{9,10},{10,1... | collective-permute-start | bytes 184328 | tf_op jit(solution)/shard_map/ppermute | solution.py:46
  26.4 22.4 %all-to-all-start = ((bf16[16,2,1920]{2,1,0:T(2,128)(2,1)}), bf16[16,2,1920]{2,1,0:T(2,128)(2,1)S(1)}, u32[]{:S(2)}, u32[]{:S(2)}) async-start(bf16[16,2,1920]{2,1,0:T(2,128)(2,1)} %reshape.356), calls=%async_computation | async-start | bytes 245760 | tf_op jit(solution)/shard_map/all_to_all | solution.py:9
  37.6 138.5 %reduce-scatter.3.cloned.1.call-start = ((), (), s32[]{:S(2)}) async-start(), calls=%async_computation.2 | async-start | bytes 1105920 | tf_op jit(solution)/shard_map/reduce_scatter | solution.py:101
  38.1 12.4 %collective-permute-start.2 = (bf16[2,4,60,256]{3,1,2,0:T(4,128)(2,1)S(1)}, bf16[2,4,60,256]{3,1,2,0:T(4,128)(2,1)S(1)}, u32[]{:S(2)}, u32[]{:S(2)}) collective-permute-start(bf16[2,4,60,256]{3,1,2,0:T(4,128)(2,1)S(1)} %pad_maximum_fusion.2), channel_id=1, source_target_pairs={{16,0},{32,16},{48,32},{17,1},{33,17},{49,33},{18,2},{34,18},{50,3... | collective-permute-start | bytes 737288 | tf_op jit(solution)/shard_map/ppermute | solution.py:23
  129.3 1.9 copy-start.3
  129.3 2.8 %copy-start.4 = (f32[2,16,1,60,256]{4,0,3,1,2:T(2,128)S(1)}, f32[2,16,1,60,256]{4,0,3,1,2:T(2,128)}, u32[]{:S(2)}) copy-start(f32[2,16,1,60,256]{4,0,3,1,2:T(2,128)} %get-tuple-element.16) | copy-start | bytes 5898244
  145.3 1.6 copy-start.1
  146.9 1.5 copy-start
  146.9 2.2 copy-start.2
  152.6 2.3 copy-start.10
  152.6 2.3 copy-start.11
  152.6 2.3 copy-start.12
  156.7 1.9 copy-start.9
  156.8 2.5 %copy-start.8 = (bf16[2,2,60,256]{3,1,2,0:T(2,128)(2,1)S(1)}, bf16[2,2,60,256]{3,1,2,0:T(2,128)(2,1)}, u32[]{:S(2)}) copy-start(bf16[2,2,60,256]{3,1,2,0:T(2,128)(2,1)} %get-tuple-element.37) | copy-start | bytes 368644
  156.8 3.9 %copy-start.7 = (bf16[2,2,60,256]{3,1,2,0:T(2,128)(2,1)S(1)}, bf16[2,2,60,256]{3,1,2,0:T(2,128)(2,1)}, u32[]{:S(2)}) copy-start(bf16[2,2,60,256]{3,1,2,0:T(2,128)(2,1)} %get-tuple-element.38) | copy-start | bytes 368644
  156.8 4.6 %copy-start.6 = (bf16[2,2,60,256]{3,1,2,0:T(2,128)(2,1)S(1)}, bf16[2,2,60,256]{3,1,2,0:T(2,128)(2,1)}, u32[]{:S(2)}) copy-start(bf16[2,2,60,256]{3,1,2,0:T(2,128)(2,1)} %get-tuple-element.31) | copy-start | bytes 368644
  157.9 69.7 %all-reduce.6.cloned.1.call-start = ((), (), s32[]{:S(2)}) async-start(), calls=%async_computation.4 | async-start | bytes 442368
Sparse Core Ops, SparseCore 0:
  21.0 87.5 all-gather.2
  158.0 18.0 reduce-scatter.2
  178.4 49.1 all-reduce.5
